TPU v7x, 32 devices: a whole 2x2x4 slice. The times are simulated.
32 devices in a mesh: row: 8 (over z, x), col: 4 (over y, core).
Axes of the slice: x: 2, y: 2, z: 4, core: 2. Of those that a mesh axis runs over, the one named last changes fastest.
Arguments:
- x_window: bfloat16 [3, 2048, 512], P(None, 'row', 'col'), may hold values from -6 to 6
- y_window: float32 [3, 2048], P(None, 'row'), may hold values from -6 to 6
- block_order: int32 [3], replicated, may hold values from 0 to 2, each once
- diag_inverse: bfloat16 [3, 2048, 2048], P(None, 'row'), may hold values from -0.5 to 1.5, as said below
- panel_window: bfloat16 [3, 2048, 2048], P(None, 'row', 'col'), may hold values from -0.078125 to 0.078125
- panel_trail: bfloat16 [1024, 3, 2048], P('row', None, 'col'), may hold values from -0.078125 to 0.078125
- x_trail: bfloat16 [1024, 512], P('row', 'col'), may hold values from -6 to 6
- y_trail: float32 [1024], P('row'), may hold values from -6 to 6
Outputs:
- whitened: bfloat16 [3, 2048, 512], P(None, 'row', 'col')
- white_resp: bfloat16 [3, 2048], P(None, 'row')
- trail_rhs: float32 [1024, 512], P('row', 'col')
- trail_resp: float32 [1024], P('row')
- normal_part: float32 [512, 512], P('row')
- right_part: float32 [512], P('row')
Inputs may be any that keep to these rules, and one draw needn't show every extreme that they name: Each diag_inverse[s] is lower triangular with a positive diagonal.
All inputs are finite; a program needn't handle non-finite values.
Results may differ from a plain program's by a relative error of at most 0.014.
Values may be sent and summed in bfloat16 or wider, within the bound.
No kernel may reach another device: no remote copies, remote signals or barrier semaphores. Data moves between devices by JAX's collectives and lax.ppermute only.
A program may use at most 64 MiB of HBM per device.

v0:
```python
import jax
import jax.numpy as jnp
from jax import lax
from jax.sharding import PartitionSpec as P


def shards(
    x_window, y_window, block_order, diag_inverse, panel_window, panel_trail, x_trail, y_trail
):
    steps = x_window.shape[0]
    own_rows = x_window.shape[1]
    own_cols = x_window.shape[2]
    width = panel_window.shape[2]
    block_rows = own_rows * lax.axis_size("row")
    full_cols = own_cols * lax.axis_size("col")
    normal_rows = full_cols // lax.axis_size("row")
    col_start = lax.axis_index("col") * width
    normal_start = lax.axis_index("row") * normal_rows
    trail_rows = x_trail.shape[0]
    solved_cols = []
    solved_resp = []
    out_tiles = []
    out_resp = []
    trail_total = jnp.zeros((trail_rows, full_cols), jnp.float32)
    trail_resp_total = jnp.zeros((trail_rows,), jnp.float32)
    gram = jnp.zeros((normal_rows, full_cols), jnp.float32)
    right = jnp.zeros((normal_rows,), jnp.float32)
    for s in range(steps):
        stored = block_order[s]
        pending = lax.dynamic_index_in_dim(x_window, stored, 0, keepdims=False).astype(jnp.float32)
        pending_resp = lax.dynamic_index_in_dim(y_window, stored, 0, keepdims=False)
        if s > 0:
            first = s * (s - 1) // 2
            factors = panel_window[first : first + s]
            earlier = jnp.stack(solved_cols)
            earlier_resp = jnp.stack(solved_resp)
            update = jnp.einsum("trw,twp->rp", factors, earlier, preferred_element_type=jnp.float32)
            update_resp = jnp.einsum(
                "trw,tw->r", factors, earlier_resp, preferred_element_type=jnp.float32
            )
            pending = pending - lax.psum_scatter(update, "col", scatter_dimension=1, tiled=True)
            pending_resp = pending_resp - lax.psum(update_resp, "col")
        residual = pending.astype(jnp.bfloat16)
        resid_resp = pending_resp.astype(jnp.bfloat16)
        whole, whole_resp = (
            lax.all_gather(residual, "row", axis=0, tiled=True),
            lax.all_gather(resid_resp, "row", axis=0, tiled=True),
        )
        inverse = diag_inverse[s]
        tile = jnp.dot(inverse, whole, preferred_element_type=jnp.float32).astype(jnp.bfloat16)
        tile_resp = jnp.dot(inverse, whole_resp, preferred_element_type=jnp.float32).astype(
            jnp.bfloat16
        )
        out_tiles.append(tile)
        out_resp.append(tile_resp)
        all_rows, all_resp = (
            lax.all_gather(tile, "row", axis=0, tiled=True),
            lax.all_gather(tile_resp, "row", axis=0, tiled=True),
        )
        mine = lax.all_to_all(all_rows, "col", split_axis=0, concat_axis=1, tiled=True)
        mine_resp = lax.dynamic_slice_in_dim(all_resp, col_start, width, 0)
        solved_cols.append(mine)
        solved_resp.append(mine_resp)
        factor_rows = panel_trail[:, s, :]
        trail_total = trail_total + jnp.dot(factor_rows, mine, preferred_element_type=jnp.float32)
        trail_resp_total = trail_resp_total + jnp.dot(
            factor_rows, mine_resp, preferred_element_type=jnp.float32
        )
        slab = lax.dynamic_slice_in_dim(mine, normal_start, normal_rows, 1)
        gram = gram + lax.dot_general(
            slab, mine, (((0,), (0,)), ((), ())), preferred_element_type=jnp.float32
        )
        right = right + lax.dot_general(
            slab, mine_resp, (((0,), (0,)), ((), ())), preferred_element_type=jnp.float32
        )
    share = lax.psum_scatter(
        trail_total.astype(jnp.bfloat16), "col", scatter_dimension=1, tiled=True
    ).astype(jnp.float32)
    trail_rhs = x_trail.astype(jnp.float32) - share
    gram, right, resp_sum = lax.psum((gram, right, trail_resp_total), "col")
    trail_resp = y_trail - resp_sum
    scale = 1.0 / (steps * block_rows)
    whitened = jnp.stack(out_tiles)
    white_resp = jnp.stack(out_resp)
    return (whitened, white_resp, trail_rhs, trail_resp, gram * scale, right * scale)


def solution(mesh):
    in_specs = (
        P(None, "row", "col"),
        P(None, "row"),
        P(),
        P(None, "row", None),
        P(None, "row", "col"),
        P("row", None, "col"),
        P("row", "col"),
        P("row"),
    )
    out_specs = (
        P(None, "row", "col"),
        P(None, "row"),
        P("row", "col"),
        P("row"),
        P("row", None),
        P("row"),
    )
    return jax.shard_map(shards, mesh=mesh, in_specs=in_specs, out_specs=out_specs, check_vma=False)
```

profile of v0, /device:TPU:0, one launch (start us, length us, event | category | flops | bytes accessed | tf_op | source)
XLA Modules:
  0.0 446.1 jit_solution(9087911912187497106)
XLA Ops:
  7.2 1.4 fusion.65
  15.3 33.2 %all-gather = bf16[1,2048,128]{2,1,0:T(8,128)(2,1)S(1)} all-gather(bf16[1,256,128]{2,1,0:T(8,128)(2,1)S(1)} %get-tuple-element.28), channel_id=2, replica_groups=mesh['row'=8,'col'=4] {'row'}, dimensions={1}, use_global_device_ids=true | all-gather | bytes 589824 | tf_op jit(solution)/shard_map/all_gather | solution.py:46
  48.5 1.7 convolution_convert_fusion.2
  50.2 31.2 %all_gather.37 = bf16[2048,128]{0,1:T(8,128)(2,1)S(1)} all-gather(bf16[256,128]{0,1:T(8,128)(2,1)S(1)} %bitcast.162), channel_id=1, replica_groups=mesh['row'=8,'col'=4] {'row'}, dimensions={0}, use_global_device_ids=true | all-gather | bytes 589824 | tf_op jit(solution)/shard_map/all_gather | solution.py:57
  82.3 3.5 all-to-all-start
  85.8 20.8 %all-gather.1 = bf16[1,2048]{1,0:T(2,128)(2,1)S(1)} all-gather(bf16[1,256]{1,0:T(2,128)(2,1)S(1)} %fusion.63), channel_id=3, replica_groups=mesh['row'=8,'col'=4] {'row'}, dimensions={1}, use_global_device_ids=true | all-gather | bytes 4608 | tf_op jit(solution)/shard_map/all_gather | solution.py:47
  106.6 1.6 fusion.15
  108.3 16.3 %all-gather.2 = bf16[8,1,256]{2,1,0:T(2,128)(2,1)S(1)} all-gather(bf16[1,1,256]{2,1,0:T(2,128)(2,1)S(1)} %reshape.44), channel_id=1, replica_groups=mesh['row'=8,'col'=4] {'row'}, dimensions={0}, use_global_device_ids=true | all-gather | bytes 4608 | tf_op jit(solution)/shard_map/all_gather | solution.py:58
  124.9 5.7 %psum.35 = f32[256]{0:T(256)S(1)} all-reduce(f32[256]{0:T(256)S(1)} %bitcast.177), channel_id=1, replica_groups=mesh['row'=8,'col'=4] {'col'}, use_global_device_ids=true, to_apply=%region_2.3 | all-reduce | flops 256 | bytes 2048 | tf_op jit(solution)/shard_map/psum | solution.py:42
  130.5 1.1 convolution_bitcast_fusion.1
  131.7 18.3 %all-gather.3 = bf16[8,1,256]{2,1,0:T(2,128)(2,1)S(1)} all-gather(bf16[1,1,256]{2,1,0:T(2,128)(2,1)S(1)} %reshape.46), channel_id=1, replica_groups=mesh['row'=8,'col'=4] {'row'}, dimensions={0}, use_global_device_ids=true | all-gather | bytes 4608 | tf_op jit(solution)/shard_map/all_gather | solution.py:47
  150.0 1.6 fusion.12
  151.7 16.3 %all-gather.4 = bf16[8,1,256]{2,1,0:T(2,128)(2,1)S(1)} all-gather(bf16[1,1,256]{2,1,0:T(2,128)(2,1)S(1)} %reshape.48), channel_id=1, replica_groups=mesh['row'=8,'col'=4] {'row'}, dimensions={0}, use_global_device_ids=true | all-gather | bytes 4608 | tf_op jit(solution)/shard_map/all_gather | solution.py:58
  168.3 5.7 %psum.36 = f32[256]{0:T(256)S(1)} all-reduce(f32[256]{0:T(256)S(1)} %bitcast.176), channel_id=1, replica_groups=mesh['row'=8,'col'=4] {'col'}, use_global_device_ids=true, to_apply=%region_3.4 | all-reduce | flops 256 | bytes 2048 | tf_op jit(solution)/shard_map/psum | solution.py:42
  174.1 18.3 %all-gather.5 = bf16[8,1,256]{2,1,0:T(2,128)(2,1)S(1)} all-gather(bf16[1,1,256]{2,1,0:T(2,128)(2,1)S(1)} %reshape.50), channel_id=1, replica_groups=mesh['row'=8,'col'=4] {'row'}, dimensions={0}, use_global_device_ids=true | all-gather | bytes 4608 | tf_op jit(solution)/shard_map/all_gather | solution.py:47
  193.4 31.7 %all_gather.38 = bf16[2048,128]{0,1:T(8,128)(2,1)S(1)} all-gather(bf16[256,128]{0,1:T(8,128)(2,1)S(1)} %fusion.34), channel_id=1, replica_groups=mesh['row'=8,'col'=4] {'row'}, dimensions={0}, use_global_device_ids=true | all-gather | bytes 589824 | tf_op jit(solution)/shard_map/all_gather | solution.py:46
  225.1 1.7 convolution_convert_fusion.1
  226.8 31.3 %all_gather.39 = bf16[2048,128]{0,1:T(8,128)(2,1)S(1)} all-gather(bf16[256,128]{0,1:T(8,128)(2,1)S(1)} %bitcast.164), channel_id=1, replica_groups=mesh['row'=8,'col'=4] {'row'}, dimensions={0}, use_global_device_ids=true | all-gather | bytes 589824 | tf_op jit(solution)/shard_map/all_gather | solution.py:57
  258.9 3.6 all-to-all-start.1
  262.5 1.6 fusion.9
  264.1 16.5 %all-gather.6 = bf16[8,1,256]{2,1,0:T(2,128)(2,1)S(1)} all-gather(bf16[1,1,256]{2,1,0:T(2,128)(2,1)S(1)} %reshape.52), channel_id=1, replica_groups=mesh['row'=8,'col'=4] {'row'}, dimensions={0}, use_global_device_ids=true | all-gather | bytes 4608 | tf_op jit(solution)/shard_map/all_gather | solution.py:58
  281.3 1.3 convolution_bitcast_fusion
  284.2 19.5 %reduce-scatter.6.cloned.1.call-done = f32[256,128]{0,1:T(8,128)} async-done(((f32[256,512]{0,1:T(8,128)}), f32[256,128]{0,1:T(8,128)}) %reduce-scatter.6.cloned.1.call-update) | async-done | bytes 131088 | tf_op jit(solution)/shard_map/reduce_scatter | solution.py:41
  304.6 31.5 %all_gather.40 = bf16[2048,128]{0,1:T(8,128)(2,1)S(1)} all-gather(bf16[256,128]{0,1:T(8,128)(2,1)S(1)} %fusion.33), channel_id=1, replica_groups=mesh['row'=8,'col'=4] {'row'}, dimensions={0}, use_global_device_ids=true | all-gather | bytes 589824 | tf_op jit(solution)/shard_map/all_gather | solution.py:46
  336.0 1.7 convolution_convert_fusion
  337.8 31.2 %all_gather.46 = bf16[2048,128]{0,1:T(8,128)(2,1)S(1)} all-gather(bf16[256,128]{0,1:T(8,128)(2,1)S(1)} %bitcast.166), channel_id=1, replica_groups=mesh['row'=8,'col'=4] {'row'}, dimensions={0}, use_global_device_ids=true | all-gather | bytes 589824 | tf_op jit(solution)/shard_map/all_gather | solution.py:57
  369.8 3.5 all-to-all-start.2
  374.6 7.4 %all-to-all-done.2 = bf16[4,512,128]{1,2,0:T(8,128)(2,1)S(1)} async-done(((bf16[4,512,128]{1,2,0:T(8,128)(2,1)}), bf16[4,512,128]{1,2,0:T(8,128)(2,1)S(1)}, u32[]{:S(2)}, u32[]{:S(2)}) %all-to-all-start.2) | async-done | bytes 524320 | tf_op jit(solution)/shard_map/all_to_all | solution.py:60
  384.2 5.7 %all-reduce = (f32[128]{0:T(128)S(1)}, f32[64]{0:T(128)S(1)}) all-reduce(f32[128]{0:T(128)S(1)} %fusion.3, f32[64]{0:T(128)S(1)} %fusion.5), channel_id=1, replica_groups=mesh['row'=8,'col'=4] {'col'}, use_global_device_ids=true, to_apply=%region_5.6 | all-reduce | flops 192 | bytes 1536 | tf_op jit(solution)/shard_map/psum | solution.py:80
  391.0 25.1 %all-reduce.3.cloned.1.call-done = f32[64,512]{1,0:T(8,128)} async-done(((f32[64,512]{1,0:T(8,128)}), f32[64,512]{1,0:T(8,128)}) %all-reduce.3.cloned.1.call-update) | async-done | bytes 131088 | tf_op jit(solution)/shard_map/psum | solution.py:80
  416.1 1.6 broadcast_multiply_fusion
  417.7 20.4 %reduce-scatter.8.cloned.1.call-done = bf16[128,128]{0,1:T(8,128)(2,1)} async-done(((bf16[128,512]{0,1:T(8,128)(2,1)}), bf16[128,128]{0,1:T(8,128)(2,1)}) %reduce-scatter.8.cloned.1.call-update) | async-done | bytes 32784 | tf_op jit(solution)/shard_map/reduce_scatter | solution.py:76
  (81 shorter events, 14.5 us)
Async XLA Ops:
  7.2 78.6 %copy-start.3 = (f32[3,256]{1,0:T(4,128)S(1)}, f32[3,256]{1,0:T(4,128)}, u32[]{:S(2)}) copy-start(f32[3,256]{1,0:T(4,128)} %param.9) | copy-start | bytes 9220
  15.3 109.4 %copy-start = (bf16[3,256,512]{2,1,0:T(8,128)(2,1)S(1)}, bf16[3,256,512]{2,1,0:T(8,128)(2,1)}, u32[]{:S(2)}) copy-start(bf16[3,256,512]{2,1,0:T(8,128)(2,1)} %param.12) | copy-start | bytes 2359300
  82.3 48.3 %all-to-all-start = ((bf16[4,512,128]{1,2,0:T(8,128)(2,1)}), bf16[4,512,128]{1,2,0:T(8,128)(2,1)S(1)}, u32[]{:S(2)}, u32[]{:S(2)}) async-start(bf16[4,512,128]{1,2,0:T(8,128)(2,1)} %bitcast.146), calls=%async_computation | async-start | bytes 1048576 | tf_op jit(solution)/shard_map/all_to_all | solution.py:60
  85.7 106.7 %reduce-scatter.4.cloned.1.call-start = ((), (), s32[]{:S(2)}) async-start(), calls=%async_computation.6 | async-start | bytes 655360 | tf_op jit(solution)/shard_map/reduce_scatter | solution.py:41
  193.3 87.4 %copy-start.2 = (bf16[128,128]{1,0:T(8,128)(2,1)S(1)}, bf16[128,128]{1,0:T(8,128)(2,1)}, u32[]{:S(2)}) copy-start(bf16[128,128]{1,0:T(8,128)(2,1)} %param.14) | copy-start | bytes 98308
  193.4 87.6 %copy-start.1 = (bf16[128,3,512]{2,0,1:T(8,128)(2,1)S(1)}, bf16[128,3,512]{2,0,1:T(8,128)(2,1)}, u32[]{:S(2)}) copy-start(bf16[128,3,512]{2,0,1:T(8,128)(2,1)} %param.13) | copy-start | bytes 1179652
  258.9 22.4 %all-to-all-start.1 = ((bf16[4,512,128]{1,2,0:T(8,128)(2,1)}), bf16[4,512,128]{1,2,0:T(8,128)(2,1)S(1)}, u32[]{:S(2)}, u32[]{:S(2)}) async-start(bf16[4,512,128]{1,2,0:T(8,128)(2,1)} %bitcast.145), calls=%async_computation.2 | async-start | bytes 1048576 | tf_op jit(solution)/shard_map/all_to_all | solution.py:60
  262.5 41.2 %reduce-scatter.6.cloned.1.call-start = ((), (), s32[]{:S(2)}) async-start(), calls=%async_computation.7 | async-start | bytes 655360 | tf_op jit(solution)/shard_map/reduce_scatter | solution.py:41
  368.9 21.6 %copy-start.4 = (f32[128]{0:T(128)S(1)}, f32[128]{0:T(128)}, u32[]{:S(2)}) copy-start(f32[128]{0:T(128)} %param.15) | copy-start | bytes 1540
  369.8 12.3 %all-to-all-start.2 = ((bf16[4,512,128]{1,2,0:T(8,128)(2,1)}), bf16[4,512,128]{1,2,0:T(8,128)(2,1)S(1)}, u32[]{:S(2)}, u32[]{:S(2)}) async-start(bf16[4,512,128]{1,2,0:T(8,128)(2,1)} %bitcast.144), calls=%async_computation.4 | async-start | bytes 1048576 | tf_op jit(solution)/shard_map/all_to_all | solution.py:60
  373.3 42.8 %all-reduce.3.cloned.1.call-start = ((), (), s32[]{:S(2)}) async-start(), calls=%async_computation.9 | async-start | bytes 262144 | tf_op jit(solution)/shard_map/psum | solution.py:80
  384.1 54.0 %reduce-scatter.8.cloned.1.call-start = ((), (), s32[]{:S(2)}) async-start(), calls=%async_computation.8 | async-start | bytes 163840 | tf_op jit(solution)/shard_map/reduce_scatter | solution.py:76
Sparse Core Ops, SparseCore 0:
  131.8 20.9 reduce-scatter.3
  282.7 20.9 reduce-scatter.5
  384.2 31.8 all-reduce.2
  418.4 19.6 reduce-scatter.7
where the time goes:
time: 447 us; the launch traced here: 446 us
  blocking collectives  314 us (70%)
  waiting for transfers between devices  72.4 us (16%)
  between operations  19.8 us (4%)
  matrix products  16.5 us (4%)
  starting transfers between devices  10.6 us (2%)
  local copies, waits for them, and re-layouts  7.06 us (2%)
  other arithmetic  5.95 us (1%)
    all_gather x3, blocking collectives, shards(): lax.all_gather(residual, 'row', axis=0, tiled=True)  96.4 us
    all_gather x3, blocking collectives, shards(): lax.all_gather(tile, 'row', axis=0, tiled=True)  93.7 us
    all_gather x3, blocking collectives, shards(): lax.all_gather(resid_resp, 'row', axis=0, tiled=True)  57.4 us
    all_gather x3, blocking collectives, shards(): lax.all_gather(tile_resp, 'row', axis=0, tiled=True)  49.1 us
    psum x1, waiting for transfers between devices, shards(): gram, right, resp_sum = lax.psum((gram, right, trail_resp_total), 'col')  25.1 us
    reduce_scatter x1, waiting for transfers between devices, shards(): lax.psum_scatter(trail_total.astype(jnp.bfloat16), 'col', scatter_dimensi...  20.4 us
    reduce_scatter x2, waiting for transfers between devices, shards(): lax.psum_scatter(update, 'col', scatter_dimension=1, tiled=True)  19.5 us
    psum x2, blocking collectives, shards(): pending_resp = pending_resp - lax.psum(update_resp, 'col')  11.3 us
  transfers between devices with their start and end apart: 7, of which 4 were waited for; matrix products, arithmetic and copies ran while one was open for 3% of the time, Pallas kernels for 0%

commit v1 on v0

--- a/solution.py
+++ b/solution.py
@@ -2,6 +2,18 @@
 import jax.numpy as jnp
 from jax import lax
 from jax.sharding import PartitionSpec as P
+
+
+def doubled_up(x, axis, dim):
+    ways, here, step = (lax.axis_size(axis), lax.axis_index(axis), x.shape[dim])
+    line, have = (x, 1)
+    while have < ways:
+        line = jnp.concatenate(
+            [line, lax.ppermute(line, axis, [(d, (d - have) % ways) for d in range(ways)])],
+            axis=dim,
+        )
+        have = 2 * have
+    return jnp.roll(line, here * step, axis=dim)
 
 
 def shards(
@@ -54,7 +66,7 @@
         out_tiles.append(tile)
         out_resp.append(tile_resp)
         all_rows, all_resp = (
-            lax.all_gather(tile, "row", axis=0, tiled=True),
+            doubled_up(tile, "row", 0),
             lax.all_gather(tile_resp, "row", axis=0, tiled=True),
         )
         mine = lax.all_to_all(all_rows, "col", split_axis=0, concat_axis=1, tiled=True)

time: 447 us -> 410 us (0.917)
  blocking collectives: 314 us -> 229 us
  waiting for transfers between devices: 72.4 us -> 110 us
  starting transfers between devices: 10.6 us -> 19 us
    all_gather x3 -> x0, blocking collectives: 93.7 us -> none  [shards(): lax.all_gather(tile, 'row', axis=0, tiled=True)]
    ppermute x0 -> x9, waiting for transfers between devices: none -> 35.9 us  [doubled_up(): lax.ppermute(line, axis, [(d, (d - have) % ways) for d in range(ways)])]
    ppermute x0 -> x9, starting transfers between devices: none -> 11.8 us  [doubled_up(): lax.ppermute(line, axis, [(d, (d - have) % ways) for d in range(ways)])]
    all_to_all x0 -> x1, blocking collectives: none -> 11.4 us  [shards(): lax.all_to_all(all_rows, 'col', split_axis=0, concat_axis=1, tiled=True)]
    all_gather x3, blocking collectives: 57.4 us -> 52 us  [shards(): lax.all_gather(resid_resp, 'row', axis=0, tiled=True)]
    all_to_all x3 -> x2, starting transfers between devices: 10.5 us -> 7.08 us  [shards(): lax.all_to_all(all_rows, 'col', split_axis=0, concat_axis=1, tiled=True)]
  transfers between devices with their start and end apart: 7 -> 15, of which waited for: 4 -> 11; matrix products, arithmetic and copies ran while one was open for 3% -> 3% of each run, Pallas kernels for 0% -> 0%
where the time goes in v1:
time: 410 us
  blocking collectives  229 us (56%)
  waiting for transfers between devices  110 us (27%)
  between operations  19.9 us (5%)
  starting transfers between devices  19 us (5%)
  matrix products  16.6 us (4%)
  other arithmetic  7.89 us (2%)
  local copies, waits for them, and re-layouts  7.5 us (2%)
    all_gather x3, blocking collectives, shards(): lax.all_gather(residual, 'row', axis=0, tiled=True)  95.9 us
    all_gather x3, blocking collectives, shards(): lax.all_gather(tile_resp, 'row', axis=0, tiled=True)  52.1 us
    all_gather x3, blocking collectives, shards(): lax.all_gather(resid_resp, 'row', axis=0, tiled=True)  52 us
    ppermute x9, waiting for transfers between devices, doubled_up(): lax.ppermute(line, axis, [(d, (d - have) % ways) for d in range(ways)])  35.9 us
    psum x1, waiting for transfers between devices, shards(): gram, right, resp_sum = lax.psum((gram, right, trail_resp_total), 'col')  25 us
    reduce_scatter x2, waiting for transfers between devices, shards(): lax.psum_scatter(update, 'col', scatter_dimension=1, tiled=True)  20.9 us
    reduce_scatter x1, waiting for transfers between devices, shards(): lax.psum_scatter(trail_total.astype(jnp.bfloat16), 'col', scatter_dimensi...  20.4 us
    ppermute x9, starting transfers between devices, doubled_up(): lax.ppermute(line, axis, [(d, (d - have) % ways) for d in range(ways)])  11.8 us
  transfers between devices with their start and end apart: 15, of which 11 were waited for; matrix products, arithmetic and copies ran while one was open for 3% of the time, Pallas kernels for 0%

profile of v1, /device:TPU:0, one launch (start us, length us, event | category | flops | bytes accessed | tf_op | source)
XLA Modules:
  0.0 409.5 jit_solution(16997572274488350236)
XLA Ops:
  15.3 33.0 %all-gather = bf16[1,2048,128]{2,1,0:T(8,128)(2,1)S(1)} all-gather(bf16[1,256,128]{2,1,0:T(8,128)(2,1)S(1)} %get-tuple-element.35), channel_id=2, replica_groups=mesh['row'=8,'col'=4] {'row'}, dimensions={1}, use_global_device_ids=true | all-gather | bytes 589824 | tf_op jit(solution)/shard_map/all_gather | solution.py:58
  48.4 1.8 convolution_convert_fusion.2
  50.2 4.4 %collective-permute-start = (bf16[256,128]{0,1:T(8,128)(2,1)S(1)}, bf16[256,128]{0,1:T(8,128)(2,1)S(1)}, u32[]{:S(2)}, u32[]{:S(2)}) collective-permute-start(bf16[256,128]{0,1:T(8,128)(2,1)S(1)} %bitcast.149), channel_id=1, source_target_pairs={{0,28},{4,0},{8,4},{12,8},{16,12},{20,16},{24,20},{28,24},{1,29},{... | collective-permute-start | bytes 196616 | tf_op jit(solution)/shard_map/ppermute | solution.py:12
  54.6 2.5 collective-permute-done
  57.4 6.9 %collective-permute-done.1 = bf16[512,128]{0,1:T(8,128)(2,1)S(1)} collective-permute-done((bf16[512,128]{0,1:T(8,128)(2,1)S(1)}, bf16[512,128]{0,1:T(8,128)(2,1)S(1)}, u32[]{:S(2)}, u32[]{:S(2)}) %collective-permute-start.1) | collective-permute-done | bytes 131104 | tf_op jit(solution)/shard_map/ppermute | solution.py:12
  64.5 9.1 %collective-permute-done.2 = bf16[1024,128]{0,1:T(8,128)(2,1)S(1)} collective-permute-done((bf16[1024,128]{0,1:T(8,128)(2,1)S(1)}, bf16[1024,128]{0,1:T(8,128)(2,1)S(1)}, u32[]{:S(2)}, u32[]{:S(2)}) %collective-permute-start.2) | collective-permute-done | bytes 262176 | tf_op jit(solution)/shard_map/ppermute | solution.py:12
  74.4 11.4 %all_to_all.54 = bf16[4,512,128]{2,1,0:T(8,128)(2,1)S(1)} all-to-all(bf16[4,512,128]{2,1,0:T(8,128)(2,1)S(1)} %bitcast.147), channel_id=1, replica_groups=mesh['row'=8,'col'=4] {'col'}, dimensions={0} | all-to-all | bytes 1048576 | tf_op jit(solution)/shard_map/all_to_all | solution.py:72
  87.3 20.9 %reduce-scatter.4.cloned.1.call-done = f32[256,128]{0,1:T(8,128)} async-done(((f32[256,512]{0,1:T(8,128)}), f32[256,128]{0,1:T(8,128)}) %reduce-scatter.4.cloned.1.call-update) | async-done | bytes 131088 | tf_op jit(solution)/shard_map/reduce_scatter | solution.py:53
  109.2 31.5 %all_gather.28 = bf16[2048,128]{0,1:T(8,128)(2,1)S(1)} all-gather(bf16[256,128]{0,1:T(8,128)(2,1)S(1)} %fusion.55), channel_id=1, replica_groups=mesh['row'=8,'col'=4] {'row'}, dimensions={0}, use_global_device_ids=true | all-gather | bytes 589824 | tf_op jit(solution)/shard_map/all_gather | solution.py:58
  140.7 1.7 convolution_convert_fusion.1
  142.4 4.3 %collective-permute-start.3 = (bf16[256,128]{0,1:T(8,128)(2,1)S(1)}, bf16[256,128]{0,1:T(8,128)(2,1)S(1)}, u32[]{:S(2)}, u32[]{:S(2)}) collective-permute-start(bf16[256,128]{0,1:T(8,128)(2,1)S(1)} %bitcast.154), channel_id=1, source_target_pairs={{0,28},{4,0},{8,4},{12,8},{16,12},{20,16},{24,20},{28,24},{1,29},{... | collective-permute-start | bytes 196616 | tf_op jit(solution)/shard_map/ppermute | solution.py:12
  146.7 16.4 %all-gather.1 = bf16[1,2048]{1,0:T(2,128)(2,1)S(1)} all-gather(bf16[1,256]{1,0:T(2,128)(2,1)S(1)} %fusion.84), channel_id=3, replica_groups=mesh['row'=8,'col'=4] {'row'}, dimensions={1}, use_global_device_ids=true | all-gather | bytes 4608 | tf_op jit(solution)/shard_map/all_gather | solution.py:59
  165.0 18.6 %all-gather.2 = bf16[8,1,256]{2,1,0:T(2,128)(2,1)S(1)} all-gather(bf16[1,1,256]{2,1,0:T(2,128)(2,1)S(1)} %reshape.44), channel_id=1, replica_groups=mesh['row'=8,'col'=4] {'row'}, dimensions={0}, use_global_device_ids=true | all-gather | bytes 4608 | tf_op jit(solution)/shard_map/all_gather | solution.py:70
  184.0 6.0 %psum.35 = f32[256]{0:T(256)S(1)} all-reduce(f32[256]{0:T(256)S(1)} %bitcast.173), channel_id=1, replica_groups=mesh['row'=8,'col'=4] {'col'}, use_global_device_ids=true, to_apply=%region_2.4 | all-reduce | flops 256 | bytes 2048 | tf_op jit(solution)/shard_map/psum | solution.py:54
  189.9 2.1 collective-permute-done.5
  193.7 3.5 all-to-all-start.1
  197.3 17.8 %all-gather.3 = bf16[8,1,256]{2,1,0:T(2,128)(2,1)S(1)} all-gather(bf16[1,1,256]{2,1,0:T(2,128)(2,1)S(1)} %reshape.46), channel_id=1, replica_groups=mesh['row'=8,'col'=4] {'row'}, dimensions={0}, use_global_device_ids=true | all-gather | bytes 4608 | tf_op jit(solution)/shard_map/all_gather | solution.py:59
  216.7 16.8 %all-gather.4 = bf16[8,1,256]{2,1,0:T(2,128)(2,1)S(1)} all-gather(bf16[1,1,256]{2,1,0:T(2,128)(2,1)S(1)} %reshape.48), channel_id=1, replica_groups=mesh['row'=8,'col'=4] {'row'}, dimensions={0}, use_global_device_ids=true | all-gather | bytes 4608 | tf_op jit(solution)/shard_map/all_gather | solution.py:70
  235.5 5.7 %psum.36 = f32[256]{0:T(256)S(1)} all-reduce(f32[256]{0:T(256)S(1)} %bitcast.172), channel_id=1, replica_groups=mesh['row'=8,'col'=4] {'col'}, use_global_device_ids=true, to_apply=%region_3.5 | all-reduce | flops 256 | bytes 2048 | tf_op jit(solution)/shard_map/psum | solution.py:54
  241.1 17.8 %all-gather.5 = bf16[8,1,256]{2,1,0:T(2,128)(2,1)S(1)} all-gather(bf16[1,1,256]{2,1,0:T(2,128)(2,1)S(1)} %reshape.50), channel_id=1, replica_groups=mesh['row'=8,'col'=4] {'row'}, dimensions={0}, use_global_device_ids=true | all-gather | bytes 4608 | tf_op jit(solution)/shard_map/all_gather | solution.py:59
  260.6 16.8 %all-gather.6 = bf16[8,1,256]{2,1,0:T(2,128)(2,1)S(1)} all-gather(bf16[1,1,256]{2,1,0:T(2,128)(2,1)S(1)} %reshape.52), channel_id=1, replica_groups=mesh['row'=8,'col'=4] {'row'}, dimensions={0}, use_global_device_ids=true | all-gather | bytes 4608 | tf_op jit(solution)/shard_map/all_gather | solution.py:70
  279.1 31.4 %all_gather.29 = bf16[2048,128]{0,1:T(8,128)(2,1)S(1)} all-gather(bf16[256,128]{0,1:T(8,128)(2,1)S(1)} %fusion.54), channel_id=1, replica_groups=mesh['row'=8,'col'=4] {'row'}, dimensions={0}, use_global_device_ids=true | all-gather | bytes 589824 | tf_op jit(solution)/shard_map/all_gather | solution.py:58
  310.5 1.7 convolution_convert_fusion
  312.2 1.6 collective-permute-start.6
  314.4 2.1 collective-permute-done.6
  317.4 4.1 %collective-permute-done.7 = bf16[512,128]{0,1:T(8,128)(2,1)S(1)} collective-permute-done((bf16[512,128]{0,1:T(8,128)(2,1)S(1)}, bf16[512,128]{0,1:T(8,128)(2,1)S(1)}, u32[]{:S(2)}, u32[]{:S(2)}) %collective-permute-start.7) | collective-permute-done | bytes 131104 | tf_op jit(solution)/shard_map/ppermute | solution.py:12
  322.2 9.0 %collective-permute-done.8 = bf16[1024,128]{0,1:T(8,128)(2,1)S(1)} collective-permute-done((bf16[1024,128]{0,1:T(8,128)(2,1)S(1)}, bf16[1024,128]{0,1:T(8,128)(2,1)S(1)}, u32[]{:S(2)}, u32[]{:S(2)}) %collective-permute-start.8) | collective-permute-done | bytes 262176 | tf_op jit(solution)/shard_map/ppermute | solution.py:12
  332.9 3.6 all-to-all-start.2
  337.8 7.5 %all-to-all-done.2 = bf16[4,512,128]{2,1,0:T(8,128)(2,1)S(1)} async-done(((bf16[4,512,128]{2,1,0:T(8,128)(2,1)}), bf16[4,512,128]{2,1,0:T(8,128)(2,1)S(1)}, u32[]{:S(2)}, u32[]{:S(2)}) %all-to-all-start.2) | async-done | bytes 524320 | tf_op jit(solution)/shard_map/all_to_all | solution.py:72
  347.8 5.7 %all-reduce = (f32[128]{0:T(128)S(1)}, f32[64]{0:T(128)S(1)}) all-reduce(f32[128]{0:T(128)S(1)} %fusion.3, f32[64]{0:T(128)S(1)} %fusion.5), channel_id=1, replica_groups=mesh['row'=8,'col'=4] {'col'}, use_global_device_ids=true, to_apply=%region_5.7 | all-reduce | flops 192 | bytes 1536 | tf_op jit(solution)/shard_map/psum | solution.py:92
  354.6 25.0 %all-reduce.3.cloned.1.call-done = f32[64,512]{1,0:T(8,128)} async-done(((f32[64,512]{1,0:T(8,128)}), f32[64,512]{1,0:T(8,128)}) %all-reduce.3.cloned.1.call-update) | async-done | bytes 131088 | tf_op jit(solution)/shard_map/psum | solution.py:92
  381.1 20.4 %reduce-scatter.8.cloned.1.call-done = bf16[128,128]{0,1:T(8,128)(2,1)} async-done(((bf16[128,512]{0,1:T(8,128)(2,1)}), bf16[128,128]{0,1:T(8,128)(2,1)}) %reduce-scatter.8.cloned.1.call-update) | async-done | bytes 32784 | tf_op jit(solution)/shard_map/reduce_scatter | solution.py:88
  (107 shorter events, 28.5 us)
Async XLA Ops:
  7.2 101.1 %reduce-scatter.4.cloned.1.call-start = ((), (), s32[]{:S(2)}) async-start(), calls=%async_computation.6 | async-start | bytes 655360 | tf_op jit(solution)/shard_map/reduce_scatter | solution.py:53
  48.4 37.7 %copy-start = (bf16[3,256,512]{2,1,0:T(8,128)(2,1)S(1)}, bf16[3,256,512]{2,1,0:T(8,128)(2,1)}, u32[]{:S(2)}) copy-start(bf16[3,256,512]{2,1,0:T(8,128)(2,1)} %param.14) | copy-start | bytes 2359300
  50.2 6.9 %collective-permute-start = (bf16[256,128]{0,1:T(8,128)(2,1)S(1)}, bf16[256,128]{0,1:T(8,128)(2,1)S(1)}, u32[]{:S(2)}, u32[]{:S(2)}) collective-permute-start(bf16[256,128]{0,1:T(8,128)(2,1)S(1)} %bitcast.149), channel_id=1, source_target_pairs={{0,28},{4,0},{8,4},{12,8},{16,12},{20,16},{24,20},{28,24},{1,29},{... | collective-permute-start | bytes 196616 | tf_op jit(solution)/shard_map/ppermute | solution.py:12
  57.1 7.3 %collective-permute-start.1 = (bf16[512,128]{0,1:T(8,128)(2,1)S(1)}, bf16[512,128]{0,1:T(8,128)(2,1)S(1)}, u32[]{:S(2)}, u32[]{:S(2)}) collective-permute-start(bf16[512,128]{0,1:T(8,128)(2,1)S(1)} %pad_maximum_fusion.4), channel_id=1, source_target_pairs={{0,24},{4,28},{8,0},{12,4},{16,8},{20,12},{24,16},{28,20},{1,25},{... | collective-permute-start | bytes 393224 | tf_op jit(solution)/shard_map/ppermute | solution.py:12
  64.4 9.2 %collective-permute-start.2 = (bf16[1024,128]{0,1:T(8,128)(2,1)S(1)}, bf16[1024,128]{0,1:T(8,128)(2,1)S(1)}, u32[]{:S(2)}, u32[]{:S(2)}) collective-permute-start(bf16[1024,128]{0,1:T(8,128)(2,1)S(1)} %pad_maximum_fusion), channel_id=1, source_target_pairs={{0,16},{4,20},{8,24},{12,28},{16,0},{20,4},{24,8},{28,12},{1,17},{... | collective-permute-start | bytes 786440 | tf_op jit(solution)/shard_map/ppermute | solution.py:12
  74.4 72.3 %copy-start.3 = (f32[3,256]{1,0:T(4,128)S(1)}, f32[3,256]{1,0:T(4,128)}, u32[]{:S(2)}) copy-start(f32[3,256]{1,0:T(4,128)} %param.11) | copy-start | bytes 9220
  142.4 20.7 %collective-permute-start.3 = (bf16[256,128]{0,1:T(8,128)(2,1)S(1)}, bf16[256,128]{0,1:T(8,128)(2,1)S(1)}, u32[]{:S(2)}, u32[]{:S(2)}) collective-permute-start(bf16[256,128]{0,1:T(8,128)(2,1)S(1)} %bitcast.154), channel_id=1, source_target_pairs={{0,28},{4,0},{8,4},{12,8},{16,12},{20,16},{24,20},{28,24},{1,29},{... | collective-permute-start | bytes 196616 | tf_op jit(solution)/shard_map/ppermute | solution.py:12
  163.1 20.6 %collective-permute-start.4 = (bf16[512,128]{0,1:T(8,128)(2,1)S(1)}, bf16[512,128]{0,1:T(8,128)(2,1)S(1)}, u32[]{:S(2)}, u32[]{:S(2)}) collective-permute-start(bf16[512,128]{0,1:T(8,128)(2,1)S(1)} %pad_maximum_fusion.5), channel_id=1, source_target_pairs={{0,24},{4,28},{8,0},{12,4},{16,8},{20,12},{24,16},{28,20},{1,25},{... | collective-permute-start | bytes 393224 | tf_op jit(solution)/shard_map/ppermute | solution.py:12
  183.7 8.3 %collective-permute-start.5 = (bf16[1024,128]{0,1:T(8,128)(2,1)S(1)}, bf16[1024,128]{0,1:T(8,128)(2,1)S(1)}, u32[]{:S(2)}, u32[]{:S(2)}) collective-permute-start(bf16[1024,128]{0,1:T(8,128)(2,1)S(1)} %pad_maximum_fusion.1), channel_id=1, source_target_pairs={{0,16},{4,20},{8,24},{12,28},{16,0},{20,4},{24,8},{28,12},{1,17},{... | collective-permute-start | bytes 786440 | tf_op jit(solution)/shard_map/ppermute | solution.py:12
  193.7 39.9 %all-to-all-start.1 = ((bf16[4,512,128]{2,1,0:T(8,128)(2,1)}), bf16[4,512,128]{2,1,0:T(8,128)(2,1)S(1)}, u32[]{:S(2)}, u32[]{:S(2)}) async-start(bf16[4,512,128]{2,1,0:T(8,128)(2,1)} %bitcast.18), calls=%async_computation.2 | async-start | bytes 1048576 | tf_op jit(solution)/shard_map/all_to_all | solution.py:72
  197.2 81.0 %reduce-scatter.6.cloned.1.call-start = ((), (), s32[]{:S(2)}) async-start(), calls=%async_computation.7 | async-start | bytes 655360 | tf_op jit(solution)/shard_map/reduce_scatter | solution.py:53
  233.6 43.9 %copy-start.2 = (bf16[128,128]{1,0:T(8,128)(2,1)S(1)}, bf16[128,128]{1,0:T(8,128)(2,1)}, u32[]{:S(2)}) copy-start(bf16[128,128]{1,0:T(8,128)(2,1)} %param.16) | copy-start | bytes 98308
  233.6 44.1 %copy-start.1 = (bf16[128,3,512]{2,0,1:T(8,128)(2,1)S(1)}, bf16[128,3,512]{2,0,1:T(8,128)(2,1)}, u32[]{:S(2)}) copy-start(bf16[128,3,512]{2,0,1:T(8,128)(2,1)} %param.15) | copy-start | bytes 1179652
  312.2 4.3 %collective-permute-start.6 = (bf16[256,128]{0,1:T(8,128)(2,1)S(1)}, bf16[256,128]{0,1:T(8,128)(2,1)S(1)}, u32[]{:S(2)}, u32[]{:S(2)}) collective-permute-start(bf16[256,128]{0,1:T(8,128)(2,1)S(1)} %bitcast.159), channel_id=1, source_target_pairs={{0,28},{4,0},{8,4},{12,8},{16,12},{20,16},{24,20},{28,24},{1,29},{... | collective-permute-start | bytes 196616 | tf_op jit(solution)/shard_map/ppermute | solution.py:12
  316.5 5.0 %collective-permute-start.7 = (bf16[512,128]{0,1:T(8,128)(2,1)S(1)}, bf16[512,128]{0,1:T(8,128)(2,1)S(1)}, u32[]{:S(2)}, u32[]{:S(2)}) collective-permute-start(bf16[512,128]{0,1:T(8,128)(2,1)S(1)} %pad_maximum_fusion.6), channel_id=1, source_target_pairs={{0,24},{4,28},{8,0},{12,4},{16,8},{20,12},{24,16},{28,20},{1,25},{... | collective-permute-start | bytes 393224 | tf_op jit(solution)/shard_map/ppermute | solution.py:12
  321.6 9.7 %collective-permute-start.8 = (bf16[1024,128]{0,1:T(8,128)(2,1)S(1)}, bf16[1024,128]{0,1:T(8,128)(2,1)S(1)}, u32[]{:S(2)}, u32[]{:S(2)}) collective-permute-start(bf16[1024,128]{0,1:T(8,128)(2,1)S(1)} %pad_maximum_fusion.2), channel_id=1, source_target_pairs={{0,16},{4,20},{8,24},{12,28},{16,0},{20,4},{24,8},{28,12},{1,17},{... | collective-permute-start | bytes 786440 | tf_op jit(solution)/shard_map/ppermute | solution.py:12
  332.9 21.2 %copy-start.4 = (f32[128]{0:T(128)S(1)}, f32[128]{0:T(128)}, u32[]{:S(2)}) copy-start(f32[128]{0:T(128)} %param.17) | copy-start | bytes 1540
  332.9 12.4 %all-to-all-start.2 = ((bf16[4,512,128]{2,1,0:T(8,128)(2,1)}), bf16[4,512,128]{2,1,0:T(8,128)(2,1)S(1)}, u32[]{:S(2)}, u32[]{:S(2)}) async-start(bf16[4,512,128]{2,1,0:T(8,128)(2,1)} %bitcast.37), calls=%async_computation.4 | async-start | bytes 1048576 | tf_op jit(solution)/shard_map/all_to_all | solution.py:72
  336.5 43.0 %all-reduce.3.cloned.1.call-start = ((), (), s32[]{:S(2)}) async-start(), calls=%async_computation.9 | async-start | bytes 262144 | tf_op jit(solution)/shard_map/psum | solution.py:92
  347.6 53.9 %reduce-scatter.8.cloned.1.call-start = ((), (), s32[]{:S(2)}) async-start(), calls=%async_computation.8 | async-start | bytes 163840 | tf_op jit(solution)/shard_map/reduce_scatter | solution.py:88
Sparse Core Ops, SparseCore 0:
  87.3 20.8 reduce-scatter.3
  235.3 20.3 reduce-scatter.5
  347.7 31.7 all-reduce.2
  381.8 19.6 reduce-scatter.7
